TPU v7x, 128 devices: a whole 4x4x4 slice. The times are simulated.
128 devices in a mesh: dp: 8 (over y_lo, x), zero: 16 (over z, y_hi, core).
Axes of the slice: x: 4, y: 4 (y_hi: 2, y_lo: 2; y = y_hi * 2 + y_lo), z: 4, core: 2. Of those that a mesh axis runs over, the one named last changes fastest.
Arguments:
- tokens: bfloat16 [16384, 1024], P(('dp', 'zero')), may hold values from -24 to 24
- cotangent: bfloat16 [16384, 1024], P(('dp', 'zero')), may hold values from -6 to 6
- segments: int32 [128, 128], P(('dp', 'zero')), may hold values from 0 to 3, never falling along the last dimension, each value on 1 to 64 neighbouring positions
- w_qkv: float32 [1024, 3072], P('zero'), may hold values from -0.1875 to 0.1875
- w_out: float32 [1024, 1024], P('zero'), may hold values from -0.75 to 0.75
- w_fc: float32 [1024, 4096], P('zero'), may hold values from -0.1875 to 0.1875
- w_proj: float32 [4096, 1024], P('zero'), may hold values from -0.09375 to 0.09375
- vectors: float32 [12, 1024], P(None, 'zero'), may hold values from -1.2 to 1.6, as said below
- mean_qkv: float32 [1024, 3072], P('zero'), may hold values from -0.6 to 0.6
- mean_out: float32 [1024, 1024], P('zero'), may hold values from -0.6 to 0.6
- mean_fc: float32 [1024, 4096], P('zero'), may hold values from -0.6 to 0.6
- mean_proj: float32 [4096, 1024], P('zero'), may hold values from -0.6 to 0.6
- mean_vectors: float32 [12, 1024], P(None, 'zero'), may hold values from -0.6 to 0.6
- square_qkv: float32 [1024, 3072], P('zero'), may hold values from 1e-05 to 0.001
- square_out: float32 [1024, 1024], P('zero'), may hold values from 1e-05 to 0.001
- square_fc: float32 [1024, 4096], P('zero'), may hold values from 1e-05 to 0.001
- square_proj: float32 [4096, 1024], P('zero'), may hold values from 1e-05 to 0.001
- square_vectors: float32 [12, 1024], P(None, 'zero'), may hold values from 1e-05 to 0.001
Outputs:
- block_out: bfloat16 [16384, 1024], P(('dp', 'zero'))
- input_grad: bfloat16 [16384, 1024], P(('dp', 'zero'))
- grad_qkv: float32 [1024, 3072], P('zero')
- grad_out: float32 [1024, 1024], P('zero')
- grad_fc: float32 [1024, 4096], P('zero')
- grad_proj: float32 [4096, 1024], P('zero')
- grad_vectors: float32 [12, 1024], P(None, 'zero')
- next_qkv: float32 [1024, 3072], P('zero')
- next_out: float32 [1024, 1024], P('zero')
- next_fc: float32 [1024, 4096], P('zero')
- next_proj: float32 [4096, 1024], P('zero')
- next_vectors: float32 [12, 1024], P(None, 'zero')
- next_mean_qkv: float32 [1024, 3072], P('zero')
- next_mean_out: float32 [1024, 1024], P('zero')
- next_mean_fc: float32 [1024, 4096], P('zero')
- next_mean_proj: float32 [4096, 1024], P('zero')
- next_mean_vectors: float32 [12, 1024], P(None, 'zero')
- next_square_qkv: float32 [1024, 3072], P('zero')
- next_square_out: float32 [1024, 1024], P('zero')
- next_square_fc: float32 [1024, 4096], P('zero')
- next_square_proj: float32 [4096, 1024], P('zero')
- next_square_vectors: float32 [12, 1024], P(None, 'zero')
Inputs may be any that keep to these rules, and one draw needn't show every extreme that they name: `segments`: in each row of 128 tokens the segment numbers never fall; each of the 4 documents of a row has 1 to 64 tokens, and one has exactly 64. `vectors`: rows 0 and 5 lie within 0.4 to 1.6; the other rows within -1.2 to 1.2.
All inputs are finite; a program needn't handle non-finite values.
Results may differ from a plain program's by a relative error of at most 0.04.
Values may be sent and summed in bfloat16 or wider, within the bound.
A program may use at most 192 MiB of HBM per device.

v0:
```python
from functools import partial
import jax
import jax.numpy as jnp
from jax import lax
from jax.sharding import PartitionSpec as P

HEADS = 16
SEQ = 128
ADAM_STEP = 3
eps_norm = 1e-05
beta_first = 0.9
beta_second = 0.999
eps_adam = 1e-08
rate_matrix = 0.02
rate_vector = 0.15
decay_matrix = 0.1


def sent_together(arrays, axis, dim, along):
    widths = [a.shape[along] for a in arrays]
    both = jnp.concatenate(arrays, axis=along)
    result = lax.all_gather(both, axis, axis=dim, tiled=True)
    return tuple(jnp.split(result, [sum(widths[:k]) for k in range(1, len(widths))], axis=along))


def in_one_piece(arrays, axis, dim, along):
    ends, at = ([], 0)
    for a in arrays[:-1]:
        at += a.shape[along]
        ends.append(at)
    both = jnp.concatenate(arrays, axis=along)
    return tuple(
        jnp.split(lax.psum_scatter(both, axis, scatter_dimension=dim, tiled=True), ends, axis=along)
    )


def gelu_tanh(inputs):
    inner = 0.7978845608028654 * (inputs + 0.044715 * inputs * inputs * inputs)
    return 0.5 * inputs * (1.0 + jnp.tanh(inner))


def layer_norm(inputs, gain_row, bias_row):
    average = jnp.mean(inputs, axis=-1, keepdims=True)
    centred = inputs - average
    variance = jnp.mean(centred * centred, axis=-1, keepdims=True)
    return centred * lax.rsqrt(variance + eps_norm) * gain_row + bias_row


def allowed_mask(seg_rows):
    length = seg_rows.shape[1]
    places = lax.iota(jnp.int32, length)
    causal = places[:, None] >= places[None, :]
    same_doc = seg_rows[:, :, None] == seg_rows[:, None, :]
    return jnp.logical_and(same_doc, causal[None])[:, None]


def attend_scores(queries, keys_in, seg_rows):
    scaling = queries.shape[-1] ** (-0.5)
    scores = (
        jnp.einsum("rqhe,rkhe->rhqk", queries, keys_in, preferred_element_type=jnp.float32)
        * scaling
    )
    return (scores, allowed_mask(seg_rows), scaling)


def attention_forward(queries, keys_in, values, seg_rows):
    scores, allowed, scaling = attend_scores(queries, keys_in, seg_rows)
    exponent = jnp.where(allowed, jnp.exp(scores), 0.0)
    log_total = jnp.log(jnp.sum(exponent, axis=-1, keepdims=True))
    attn_weights = jnp.where(allowed, jnp.exp(scores - log_total), 0.0).astype(jnp.bfloat16)
    attended = jnp.einsum(
        "rhqk,rkhe->rqhe", attn_weights, values, preferred_element_type=jnp.float32
    )
    return (attended.astype(jnp.bfloat16), log_total)


def attention_backward(queries, keys_in, values, seg_rows, log_total, grad_att):
    scores, allowed, scaling = attend_scores(queries, keys_in, seg_rows)
    weights_full = jnp.where(allowed, jnp.exp(scores - log_total), 0.0)
    weights_half = weights_full.astype(jnp.bfloat16)
    grad_values = jnp.einsum(
        "rhqk,rqhe->rkhe", weights_half, grad_att, preferred_element_type=jnp.float32
    )
    grad_weights = jnp.einsum(
        "rqhe,rkhe->rhqk", grad_att, values, preferred_element_type=jnp.float32
    )
    row_dot = jnp.sum(weights_full * grad_weights, axis=-1, keepdims=True)
    grad_scores = (weights_full * (grad_weights - row_dot) * scaling).astype(jnp.bfloat16)
    grad_queries = jnp.einsum(
        "rhqk,rkhe->rqhe", grad_scores, keys_in, preferred_element_type=jnp.float32
    )
    grad_keys = jnp.einsum(
        "rhqk,rqhe->rkhe", grad_scores, queries, preferred_element_type=jnp.float32
    )
    return (grad_queries, grad_keys, grad_values)


def block_pass(tokens_in, cot_in, seg_rows, qkv_mat, out_mat, fc_mat, proj_mat, vec_rows):
    count_tok = tokens_in.shape[0]
    width = tokens_in.shape[1]
    head_width = width // HEADS
    row_count = count_tok // SEQ
    split_shape = (row_count, SEQ, HEADS, head_width)
    tokens32 = tokens_in.astype(jnp.float32)
    normed_one = layer_norm(tokens32, vec_rows[0], vec_rows[1]).astype(jnp.bfloat16)
    projected = jnp.dot(normed_one, qkv_mat, preferred_element_type=jnp.float32)
    queries = (projected[:, :width] + vec_rows[2]).astype(jnp.bfloat16).reshape(split_shape)
    keys_in = projected[:, width : 2 * width].astype(jnp.bfloat16).reshape(split_shape)
    values = (projected[:, 2 * width :] + vec_rows[3]).astype(jnp.bfloat16).reshape(split_shape)
    attended, log_total = attention_forward(queries, keys_in, values, seg_rows)
    attended = attended.reshape(count_tok, width)
    middle = tokens32 + jnp.dot(attended, out_mat, preferred_element_type=jnp.float32) + vec_rows[4]
    normed_two = layer_norm(middle, vec_rows[5], vec_rows[6]).astype(jnp.bfloat16)
    fc_bias = vec_rows[8:].reshape(-1)
    hidden_pre = jnp.dot(normed_two, fc_mat, preferred_element_type=jnp.float32) + fc_bias
    hidden = gelu_tanh(hidden_pre).astype(jnp.bfloat16)
    block_out = (
        middle + jnp.dot(hidden, proj_mat, preferred_element_type=jnp.float32) + vec_rows[7]
    ).astype(jnp.bfloat16)
    cot32 = cot_in.astype(jnp.float32)
    grad_proj = jnp.dot(hidden.T, cot_in, preferred_element_type=jnp.float32)
    grad_hidden = jnp.dot(cot_in, proj_mat.T, preferred_element_type=jnp.float32)
    gelu_back = jax.vjp(gelu_tanh, hidden_pre)[1]
    grad_pre = gelu_back(grad_hidden)[0]
    grad_pre_half = grad_pre.astype(jnp.bfloat16)
    grad_fc = jnp.dot(normed_two.T, grad_pre_half, preferred_element_type=jnp.float32)
    grad_normed_two = jnp.dot(grad_pre_half, fc_mat.T, preferred_element_type=jnp.float32)
    norm_two_back = jax.vjp(layer_norm, middle, vec_rows[5], vec_rows[6])[1]
    grad_mid_norm, grad_gain_two, grad_bias_two = norm_two_back(grad_normed_two)
    grad_middle = cot32 + grad_mid_norm
    grad_middle_half = grad_middle.astype(jnp.bfloat16)
    grad_out = jnp.dot(attended.T, grad_middle_half, preferred_element_type=jnp.float32)
    grad_attended = jnp.dot(grad_middle_half, out_mat.T, preferred_element_type=jnp.float32)
    grad_attended = grad_attended.astype(jnp.bfloat16).reshape(split_shape)
    grad_queries, grad_keys, grad_values = attention_backward(
        queries, keys_in, values, seg_rows, log_total, grad_attended
    )
    flat_queries = grad_queries.reshape(count_tok, width)
    flat_keys = grad_keys.reshape(count_tok, width)
    flat_values = grad_values.reshape(count_tok, width)
    grad_projected = jnp.concatenate([flat_queries, flat_keys, flat_values], axis=1).astype(
        jnp.bfloat16
    )
    grad_qkv = jnp.dot(normed_one.T, grad_projected, preferred_element_type=jnp.float32)
    grad_normed_one = jnp.dot(grad_projected, qkv_mat.T, preferred_element_type=jnp.float32)
    norm_one_back = jax.vjp(layer_norm, tokens32, vec_rows[0], vec_rows[1])[1]
    grad_tok_norm, grad_gain_one, grad_bias_one = norm_one_back(grad_normed_one)
    input_grad = (grad_middle + grad_tok_norm).astype(jnp.bfloat16)
    small_rows = jnp.stack(
        [
            grad_gain_one,
            grad_bias_one,
            jnp.sum(flat_queries, axis=0),
            jnp.sum(flat_values, axis=0),
            jnp.sum(grad_middle, axis=0),
            grad_gain_two,
            grad_bias_two,
            jnp.sum(cot32, axis=0),
        ]
    )
    grad_vec = jnp.concatenate([small_rows, jnp.sum(grad_pre, axis=0).reshape(-1, width)], axis=0)
    return (block_out, input_grad, (grad_qkv, grad_out, grad_fc, grad_proj, grad_vec))


def adam_step(weight, gradient, mean_old, square_old, rate, decay):
    mean_new = beta_first * mean_old + (1.0 - beta_first) * gradient
    square_new = beta_second * square_old + (1.0 - beta_second) * gradient * gradient
    mean_hat = mean_new / (1.0 - beta_first**ADAM_STEP)
    square_hat = square_new / (1.0 - beta_second**ADAM_STEP)
    weight_new = weight - rate * (mean_hat / (jnp.sqrt(square_hat) + eps_adam) + decay * weight)
    return (weight_new, mean_new, square_new)


def local(
    tokens,
    cotangent,
    segments,
    w_qkv,
    w_out,
    w_fc,
    w_proj,
    vectors,
    mean_qkv,
    mean_out,
    mean_fc,
    mean_proj,
    mean_vectors,
    square_qkv,
    square_out,
    square_fc,
    square_proj,
    square_vectors,
):
    dp_size = lax.axis_size("dp")
    zero_size = lax.axis_size("zero")
    replicas = dp_size * zero_size
    qkv_mat, out_mat, fc_mat, proj_mat, vec_half = (
        *sent_together(
            (w_qkv.astype(jnp.bfloat16), w_out.astype(jnp.bfloat16), w_fc.astype(jnp.bfloat16)),
            "zero",
            0,
            1,
        ),
        lax.all_gather(w_proj.astype(jnp.bfloat16), "zero", axis=0, tiled=True),
        lax.all_gather(vectors.astype(jnp.bfloat16), "zero", axis=1, tiled=True),
    )
    vec_rows = vec_half.astype(jnp.float32)
    block_out, input_grad, local_grads = block_pass(
        tokens, cotangent, segments, qkv_mat, out_mat, fc_mat, proj_mat, vec_rows
    )
    pieces = (
        *tuple(
            (
                part.astype(jnp.float32)
                for part in in_one_piece(
                    (
                        local_grads[0].astype(jnp.bfloat16),
                        local_grads[1].astype(jnp.bfloat16),
                        local_grads[2].astype(jnp.bfloat16),
                    ),
                    "zero",
                    0,
                    1,
                )
            )
        ),
        lax.psum_scatter(
            local_grads[3].astype(jnp.bfloat16), "zero", scatter_dimension=0, tiled=True
        ).astype(jnp.float32),
        lax.psum_scatter(
            local_grads[4].astype(jnp.bfloat16), "zero", scatter_dimension=1, tiled=True
        ).astype(jnp.float32),
    )
    summed = (
        lax.psum(pieces[0].astype(jnp.bfloat16), "dp").astype(jnp.float32),
        lax.psum(pieces[1].astype(jnp.bfloat16), "dp").astype(jnp.float32),
        lax.psum(pieces[2].astype(jnp.bfloat16), "dp").astype(jnp.float32),
        lax.psum(pieces[3].astype(jnp.bfloat16), "dp").astype(jnp.float32),
        lax.psum(pieces[4].astype(jnp.bfloat16), "dp").astype(jnp.float32),
    )
    grads = jax.tree.map(partial(jnp.multiply, 1.0 / replicas), summed)
    first = adam_step(w_qkv, grads[0], mean_qkv, square_qkv, rate_matrix, decay_matrix)
    second = adam_step(w_out, grads[1], mean_out, square_out, rate_matrix, decay_matrix)
    third = adam_step(w_fc, grads[2], mean_fc, square_fc, rate_matrix, decay_matrix)
    fourth = adam_step(w_proj, grads[3], mean_proj, square_proj, rate_matrix, decay_matrix)
    fifth = adam_step(vectors, grads[4], mean_vectors, square_vectors, rate_vector, 0.0)
    return (
        block_out,
        input_grad,
        grads[0],
        grads[1],
        grads[2],
        grads[3],
        grads[4],
        first[0],
        second[0],
        third[0],
        fourth[0],
        fifth[0],
        first[1],
        second[1],
        third[1],
        fourth[1],
        fifth[1],
        first[2],
        second[2],
        third[2],
        fourth[2],
        fifth[2],
    )


def solution(mesh):
    placed = (
        P(("dp", "zero"), None),
        P(("dp", "zero"), None),
        P(("dp", "zero"), None),
        P("zero", None),
        P("zero", None),
        P("zero", None),
        P("zero", None),
        P(None, "zero"),
        P("zero", None),
        P("zero", None),
        P("zero", None),
        P("zero", None),
        P(None, "zero"),
        P("zero", None),
        P("zero", None),
        P("zero", None),
        P("zero", None),
        P(None, "zero"),
    )
    return jax.shard_map(
        local,
        mesh=mesh,
        in_specs=placed,
        out_specs=(
            P(("dp", "zero"), None),
            P(("dp", "zero"), None),
            P("zero", None),
            P("zero", None),
            P("zero", None),
            P("zero", None),
            P(None, "zero"),
            P("zero", None),
            P("zero", None),
            P("zero", None),
            P("zero", None),
            P(None, "zero"),
            P("zero", None),
            P("zero", None),
            P("zero", None),
            P("zero", None),
            P(None, "zero"),
            P("zero", None),
            P("zero", None),
            P("zero", None),
            P("zero", None),
            P(None, "zero"),
        ),
        check_vma=False,
    )
```

profile of v0, /device:TPU:0, one launch (start us, length us, event | category | flops | bytes accessed | tf_op | source)
XLA Modules:
  0.0 683.3 jit_solution(5639549732843436723)
XLA Ops:
  7.3 2.2 convert_element_type.127
  9.8 1.0 pad_maximum_fusion.1
  10.9 26.1 %all-gather = bf16[16,64,12]{1,2,0:T(8,128)(2,1)S(1)} all-gather(bf16[1,64,12]{1,2,0:T(8,128)(2,1)S(1)} %convert_bitcast_fusion), channel_id=1, replica_groups=mesh['dp'=8,'zero'=16] {'zero'}, dimensions={0}, use_global_device_ids=true | all-gather | bytes 26112 | tf_op jit(solution)/shard_map/all_gather | solution.py:205
  37.0 0.1 reshape.283
  37.1 0.1 convert_reduce_fusion
  37.3 0.2 fusion.67
  37.5 0.1 fusion.84
  37.6 49.3 %all-gather.6.cloned.1.call-done = bf16[4096,1024]{1,0:T(8,128)(2,1)} async-done(((bf16[256,1024]{1,0:T(8,128)(2,1)}), bf16[4096,1024]{1,0:T(8,128)(2,1)}) %all-gather.6.cloned.1.call-update) | async-done | bytes 8388624 | tf_op jit(solution)/shard_map/all_gather | solution.py:204
  86.9 6.2 fusion.127
  93.2 103.9 %all-gather.4.cloned.1.call-done = bf16[1024,8192]{1,0:T(8,128)(2,1)} async-done(((bf16[64,8192]{1,0:T(8,128)(2,1)}), bf16[1024,8192]{1,0:T(8,128)(2,1)}) %all-gather.4.cloned.1.call-update) | async-done | bytes 16777232 | tf_op jit(solution)/shard_map/all_gather | solution.py:22
  197.1 3.9 fusion.8
  201.0 0.8 fusion.69
  201.8 0.8 copy.75
  202.6 0.2 copy.76
  202.8 1.2 copy.74
  204.1 1.4 convolution_multiply_fusion
  205.5 1.0 copy-done.18
  206.4 1.3 fusion.30
  207.7 2.7 convolution_convert_fusion.5
  210.5 2.2 fusion.124
  212.7 0.2 multiply_reduce_fusion.3
  212.9 7.9 %fusion.118 = (bf16[4096]{0:T(1024)(128)(2,1)S(1)}, bf16[128,4096]{1,0:T(8,128)(2,1)S(1)}, f32[128,4096]{1,0:T(8,128)}) fusion(f32[128,4096]{1,0:T(8,128)S(1)} %fusion.127, f32[4096]{0:T(1024)S(1)} %bitcast.99, bf16[1024,8192]{1,0:T(8,128)(2,1)} %all-gather.4.cloned.1.call-done, f32[128,1024]{1,0:T(8,128)S(1)} %get-tuple-element.74, ...), kind=kOutput, calls=%fused_computation.155 | convolution fusion | flops 1088024576 | bytes 14189568 | tf_op jit(solution)/shard_map/dot_general | solution.py:115
  220.9 6.8 multiply_reduce_fusion.1
  227.7 0.3 fusion.120
  228.0 2.6 fusion.40
  230.6 0.2 copy.78
  230.8 0.7 copy-done.24
  231.5 3.0 fusion.121
  234.4 1.4 fusion.128
  235.8 1.0 copy-done.19
  236.8 2.8 convolution_convert_fusion.4
  239.6 3.4 fusion.122
  243.0 3.2 convolution_convert_fusion.3
  246.1 5.7 convolution_convert_fusion.1
  251.8 2.9 copy.82
  254.7 3.2 convolution_convert_fusion.2
  257.9 0.4 copy-done
  258.3 6.6 pad_maximum_fusion
  265.0 1.5 copy-done.3
  266.5 6.2 convolution_convert_fusion
  272.8 0.1 stack.25
  272.9 0.1 stack.24
  273.0 6.6 fusion.107
  279.6 0.3 fusion.66
  280.0 1.0 fusion.104
  281.1 0.9 copy.87
  282.0 0.3 all-reduce.3.cloned.1.call-start
  282.3 127.4 %reduce-scatter.6.cloned.1.call-done = bf16[64,8192]{1,0:T(8,128)(2,1)} async-done(((bf16[1024,8192]{1,0:T(8,128)(2,1)}), bf16[64,8192]{1,0:T(8,128)(2,1)}) %reduce-scatter.6.cloned.1.call-update) | async-done | bytes 1048592 | tf_op jit(solution)/shard_map/reduce_scatter | solution.py:33
  409.6 1.6 split.28
  411.2 1.8 split.27
  413.0 1.9 split.29
  414.9 99.2 %reduce-scatter.8.cloned.1.call-done = bf16[256,1024]{1,0:T(8,128)(2,1)} async-done(((bf16[4096,1024]{1,0:T(8,128)(2,1)}), bf16[256,1024]{1,0:T(8,128)(2,1)}) %reduce-scatter.8.cloned.1.call-update) | async-done | bytes 524304 | tf_op jit(solution)/shard_map/reduce_scatter | solution.py:227
  514.1 5.6 fusion.39
  519.7 62.4 %reduce-scatter.10.cloned.1.call-done = bf16[64,12]{1,0:T(8,128)(2,1)} async-done(((bf16[1024,12]{1,0:T(8,128)(2,1)}), bf16[64,12]{1,0:T(8,128)(2,1)}) %reduce-scatter.10.cloned.1.call-update) | async-done | bytes 1552
  582.0 0.8 copy.88
  582.8 19.0 %psum.39 = bf16[12,64]{1,0:T(8,128)(2,1)S(1)} all-reduce(bf16[12,64]{1,0:T(8,128)(2,1)S(1)} %copy.88), channel_id=1, replica_groups=mesh['dp'=8,'zero'=16] {'dp'}, use_global_device_ids=true, to_apply=%region_26.27 | all-reduce | flops 768 | bytes 3072 | tf_op jit(solution)/shard_map/psum | solution.py:239
  601.8 0.6 multiply_subtract_fusion.4
  602.5 62.1 %all-reduce.3.cloned.1.call-done = (bf16[64,3072]{1,0:T(8,128)(2,1)}, bf16[64,1024]{1,0:T(8,128)(2,1)}, bf16[64,4096]{1,0:T(8,128)(2,1)}, bf16[256,1024]{1,0:T(8,128)(2,1)}) async-done(((bf16[64,3072]{1,0:T(8,128)(2,1)}, bf16[64,1024]{1,0:T(8,128)(2,1)}, bf16[64,4096]{1,0:T(8,128)(2,1)}, bf16[256,1024]{1,0:T(8,128)(2,1)}), (bf16[64,3072]{1,0:T(8,128)(2,1)}, bf16[64,1024]{1,0:T(8,128)(2,1)}, ...) | async-done | bytes 1572880 | tf_op jit(solution)/shard_map/psum | solution.py:235
  664.6 2.2 multiply_subtract_fusion.3
  666.9 3.4 multiply_subtract_fusion.2
  670.4 2.6 multiply_subtract_fusion.1
  673.0 0.2 copy-done.14
  673.3 0.5 copy-done.26
  673.8 2.7 multiply_subtract_fusion
  (96 shorter events, 0.9 us)
Async XLA Ops:
  7.2 2.4 copy-start.17
  7.2 2.4 copy-start.9
  7.2 2.5 copy-start.6
  7.2 79.7 %all-gather.6.cloned.1.call-start = ((), (), s32[]{:S(2)}) async-start(), calls=%async_computation.4 | async-start | bytes 8912896 | tf_op jit(solution)/shard_map/all_gather | solution.py:204
  9.5 187.5 %all-gather.4.cloned.1.call-start = ((), (), s32[]{:S(2)}) async-start(), calls=%async_computation.3 | async-start | bytes 17825792 | tf_op jit(solution)/shard_map/all_gather | solution.py:22
  9.7 1.2 copy-start.29
  9.8 27.4 %copy-start.1 = (bf16[128,1024]{1,0:T(8,128)(2,1)S(1)}, bf16[128,1024]{1,0:T(8,128)(2,1)}, u32[]{:S(2)}) copy-start(bf16[128,1024]{1,0:T(8,128)(2,1)} %param.18) | copy-start | bytes 786436
  9.8 27.7 %copy-start.32 = (s32[1,128]{1,0:T(1,128)S(1)}, s32[1,128]{1,0:T(1,128)}, u32[]{:S(2)}) copy-start(s32[1,128]{1,0:T(1,128)} %param.20) | copy-start | bytes 1540
  9.8 77.2 %copy-start.2 = (bf16[128,1024]{1,0:T(8,128)(2,1)S(1)}, bf16[128,1024]{1,0:T(8,128)(2,1)}, u32[]{:S(2)}) copy-start(bf16[128,1024]{1,0:T(8,128)(2,1)} %param.19) | copy-start | bytes 786436
  10.9 398.8 %reduce-scatter.6.cloned.1.call-start = ((), (), s32[]{:S(2)}) async-start(), calls=%async_computation.5 | async-start | bytes 17825792 | tf_op jit(solution)/shard_map/reduce_scatter | solution.py:33
  202.8 4.9 copy-start.20
  204.0 6.4 copy-start.23
  205.5 1.0 copy-start.18
  220.9 6.8 copy-start.15
  227.9 15.0 %copy-start.4 = (f32[128,1024]{1,0:T(8,128)}, f32[128,1024]{1,0:T(8,128)S(1)}, u32[]{:S(2)}) copy-start(f32[128,1024]{1,0:T(8,128)S(1)} %get-tuple-element.56) | copy-start | bytes 1572868
  230.6 6.2 copy-start.22
  230.8 0.7 copy-start.24
  231.5 8.1 %copy-start.21 = (bf16[128,1024]{0,1:T(8,128)(2,1)S(1)}, bf16[128,1024]{0,1:T(8,128)(2,1)}, u32[]{:S(2)}) copy-start(bf16[128,1024]{0,1:T(8,128)(2,1)} %copy-done.20) | copy-start | bytes 786436
  235.8 1.0 copy-start.19
  239.6 6.5 copy-start.16
  254.7 3.6 copy-start
  264.9 1.6 copy-start.3
  264.9 249.1 %reduce-scatter.8.cloned.1.call-start = ((), (), s32[]{:S(2)}) async-start(), calls=%async_computation.6 | async-start | bytes 8912896 | tf_op jit(solution)/shard_map/reduce_scatter | solution.py:227
  272.7 309.3 %reduce-scatter.10.cloned.1.call-start = ((), (), s32[]{:S(2)}) async-start(), calls=%async_computation.7 | async-start | bytes 278528
  273.0 6.9 %copy-start.5 = (f32[128,1024]{1,0:T(8,128)S(1)}, f32[128,1024]{1,0:T(8,128)}, u32[]{:S(2)}) copy-start(f32[128,1024]{1,0:T(8,128)} %copy-done.4) | copy-start | bytes 1572868
  282.0 382.6 %all-reduce.3.cloned.1.call-start = ((), (), s32[]{:S(2)}) async-start(), calls=%async_computation.8 | async-start | bytes 3145728 | tf_op jit(solution)/shard_map/psum | solution.py:235
  514.0 87.8 %copy-start.30 = (f32[12,64]{1,0:T(8,128)S(1)}, f32[12,64]{1,0:T(8,128)}, u32[]{:S(2)}) copy-start(f32[12,64]{1,0:T(8,128)} %param.30) | copy-start | bytes 9220
  514.0 87.8 %copy-start.31 = (f32[12,64]{1,0:T(8,128)S(1)}, f32[12,64]{1,0:T(8,128)}, u32[]{:S(2)}) copy-start(f32[12,64]{1,0:T(8,128)} %param.35) | copy-start | bytes 9220
  519.7 147.2 %copy-start.10 = (f32[64,3072]{1,0:T(8,128)S(1)}, f32[64,3072]{1,0:T(8,128)}, u32[]{:S(2)}) copy-start(f32[64,3072]{1,0:T(8,128)} %param.21) | copy-start | bytes 2359300
  519.7 147.2 %copy-start.25 = (f32[64,3072]{1,0:T(8,128)S(1)}, f32[64,3072]{1,0:T(8,128)}, u32[]{:S(2)}) copy-start(f32[64,3072]{1,0:T(8,128)} %param.26) | copy-start | bytes 2359300
  664.6 2.3 copy-start.28
  666.9 3.5 copy-start.7
  666.9 3.4 copy-start.11
  666.9 3.4 copy-start.12
  666.9 3.4 copy-start.27
  670.3 2.7 copy-start.8
  670.4 2.7 copy-start.13
  670.4 2.9 copy-start.14
  670.4 3.4 copy-start.26
Sparse Core Ops, SparseCore 0:
  11.1 75.7 all-gather.5
  90.0 107.0 all-gather.3
  265.0 144.5 reduce-scatter.5
  413.8 100.1 reduce-scatter.7
  518.1 63.8 reduce-scatter.9
  585.8 78.7 all-reduce.2
where the time goes:
time: 684 us; the launch traced here: 683 us
  waiting for transfers between devices  504 us (74%)
  matrix products  74.7 us (11%)
  blocking collectives  45.1 us (7%)
  other arithmetic  26.1 us (4%)
  local copies, waits for them, and re-layouts  18 us (3%)
  between operations  14.6 us (2%)
    reduce_scatter x1, waiting for transfers between devices, in_one_piece(): lax.psum_scatter(both, axis, scatter_dimension=dim, tiled=True)  127 us
    all_gather x1, waiting for transfers between devices, sent_together(): result = lax.all_gather(both, axis, axis=dim, tiled=True)  104 us
    reduce_scatter x1, waiting for transfers between devices, local(): lax.psum_scatter(local_grads[3].astype(jnp.bfloat16), 'zero', scatter_dim...  99.2 us
    unnamed x7, waiting for transfers between devices  62.5 us
    psum x1, waiting for transfers between devices, local(): lax.psum(pieces[0].astype(jnp.bfloat16), 'dp').astype(jnp.float32)  62.1 us
    all_gather x1, waiting for transfers between devices, local(): lax.all_gather(w_proj.astype(jnp.bfloat16), 'zero', axis=0, tiled=True)  49.3 us
    all_gather x1, blocking collectives, local(): lax.all_gather(vectors.astype(jnp.bfloat16), 'zero', axis=1, tiled=True)  26.1 us
    psum x1, blocking collectives, local(): lax.psum(pieces[4].astype(jnp.bfloat16), 'dp').astype(jnp.float32)  19 us
  transfers between devices with their start and end apart: 6, of which 6 were waited for; matrix products, arithmetic and copies ran while one was open for 5% of the time, Pallas kernels for 0%

commit v1 on v0

--- a/solution.py
+++ b/solution.py
@@ -232,7 +232,7 @@
         ).astype(jnp.float32),
     )
     summed = (
-        lax.psum(pieces[0].astype(jnp.bfloat16), "dp").astype(jnp.float32),
+        jnp.sum(lax.all_gather(pieces[0].astype(jnp.bfloat16), "dp"), axis=0).astype(jnp.float32),
         lax.psum(pieces[1].astype(jnp.bfloat16), "dp").astype(jnp.float32),
         lax.psum(pieces[2].astype(jnp.bfloat16), "dp").astype(jnp.float32),
         lax.psum(pieces[3].astype(jnp.bfloat16), "dp").astype(jnp.float32),

time: 684 us -> 721 us (1.054)
  waiting for transfers between devices: 504 us -> 539 us
    all_gather x0 -> x1, waiting for transfers between devices: none -> 36.7 us  [local(): lax.all_gather(pieces[0].astype(jnp.bfloat16), 'dp')]
    unnamed x7 -> x8, waiting for transfers between devices: 62.5 us -> 60.4 us
  transfers between devices with their start and end apart: 6 -> 7, of which waited for: 6 -> 7; matrix products, arithmetic and copies ran while one was open for 5% -> 6% of each run, Pallas kernels for 0% -> 0%
where the time goes in v1:
time: 721 us; the launch traced here: 720 us
  waiting for transfers between devices  539 us (75%)
  matrix products  74.7 us (10%)
  blocking collectives  45.1 us (6%)
  other arithmetic  28.9 us (4%)
  local copies, waits for them, and re-layouts  17.2 us (2%)
  between operations  14.7 us (2%)
    reduce_scatter x1, waiting for transfers between devices, in_one_piece(): lax.psum_scatter(both, axis, scatter_dimension=dim, tiled=True)  128 us
    all_gather x1, waiting for transfers between devices, sent_together(): result = lax.all_gather(both, axis, axis=dim, tiled=True)  104 us
    reduce_scatter x1, waiting for transfers between devices, local(): lax.psum_scatter(local_grads[3].astype(jnp.bfloat16), 'zero', scatter_dim...  101 us
    unnamed x8, waiting for transfers between devices  60.4 us
    psum x1, waiting for transfers between devices, local(): lax.psum(pieces[1].astype(jnp.bfloat16), 'dp').astype(jnp.float32)  60.1 us
    all_gather x1, waiting for transfers between devices, local(): lax.all_gather(w_proj.astype(jnp.bfloat16), 'zero', axis=0, tiled=True)  49.3 us
    all_gather x1, waiting for transfers between devices, local(): lax.all_gather(pieces[0].astype(jnp.bfloat16), 'dp')  36.7 us
    all_gather x1, blocking collectives, local(): lax.all_gather(vectors.astype(jnp.bfloat16), 'zero', axis=1, tiled=True)  26.1 us
  transfers between devices with their start and end apart: 7, of which 7 were waited for; matrix products, arithmetic and copies ran while one was open for 6% of the time, Pallas kernels for 0%

profile of v1, /device:TPU:0, one launch (start us, length us, event | category | flops | bytes accessed | tf_op | source)
XLA Modules:
  0.0 720.0 jit_solution(3183698781178678207)
XLA Ops:
  7.3 2.2 convert_element_type.129
  9.8 1.0 pad_maximum_fusion.1
  10.9 26.1 %all-gather.1 = bf16[16,64,12]{1,2,0:T(8,128)(2,1)S(1)} all-gather(bf16[1,64,12]{1,2,0:T(8,128)(2,1)S(1)} %convert_bitcast_fusion), channel_id=1, replica_groups=mesh['dp'=8,'zero'=16] {'zero'}, dimensions={0}, use_global_device_ids=true | all-gather | bytes 26112 | tf_op jit(solution)/shard_map/all_gather | solution.py:205
  37.0 0.1 reshape.284
  37.1 0.1 convert_reduce_fusion
  37.3 0.2 fusion.67
  37.5 0.1 fusion.84
  37.6 49.3 %all-gather.8.cloned.1.call-done = bf16[4096,1024]{1,0:T(8,128)(2,1)} async-done(((bf16[256,1024]{1,0:T(8,128)(2,1)}), bf16[4096,1024]{1,0:T(8,128)(2,1)}) %all-gather.8.cloned.1.call-update) | async-done | bytes 8388624 | tf_op jit(solution)/shard_map/all_gather | solution.py:204
  86.9 6.2 fusion.127
  93.2 103.9 %all-gather.6.cloned.1.call-done = bf16[1024,8192]{1,0:T(8,128)(2,1)} async-done(((bf16[64,8192]{1,0:T(8,128)(2,1)}), bf16[1024,8192]{1,0:T(8,128)(2,1)}) %all-gather.6.cloned.1.call-update) | async-done | bytes 16777232 | tf_op jit(solution)/shard_map/all_gather | solution.py:22
  197.1 3.9 fusion.8
  201.0 0.8 fusion.69
  201.8 0.8 copy.75
  202.6 0.2 copy.76
  202.8 1.2 copy.74
  204.1 1.4 convolution_multiply_fusion
  205.5 1.0 copy-done.16
  206.4 1.3 fusion.30
  207.7 2.7 convolution_convert_fusion.5
  210.5 2.2 fusion.124
  212.7 0.2 multiply_reduce_fusion.3
  212.9 7.9 %fusion.118 = (bf16[4096]{0:T(1024)(128)(2,1)S(1)}, bf16[128,4096]{1,0:T(8,128)(2,1)S(1)}, f32[128,4096]{1,0:T(8,128)}) fusion(f32[128,4096]{1,0:T(8,128)S(1)} %fusion.127, f32[4096]{0:T(1024)S(1)} %bitcast.101, bf16[1024,8192]{1,0:T(8,128)(2,1)} %all-gather.6.cloned.1.call-done, f32[128,1024]{1,0:T(8,128)S(1)} %get-tuple-element.73, ...), kind=kOutput, calls=%fused_computation.155 | convolution fusion | flops 1088024576 | bytes 14189568 | tf_op jit(solution)/shard_map/dot_general | solution.py:115
  220.9 6.8 multiply_reduce_fusion.1
  227.7 0.3 fusion.120
  228.0 2.6 fusion.40
  230.6 0.2 copy.78
  230.8 0.7 copy-done.22
  231.5 3.0 fusion.121
  234.4 1.4 fusion.128
  235.8 1.0 copy-done.17
  236.8 2.8 convolution_convert_fusion.4
  239.6 3.4 fusion.122
  243.0 3.2 convolution_convert_fusion.3
  246.1 5.7 convolution_convert_fusion.1
  251.8 2.9 copy.82
  254.7 3.2 convolution_convert_fusion.2
  257.9 0.4 copy-done
  258.3 6.6 pad_maximum_fusion
  265.0 1.5 copy-done.3
  266.5 6.2 convolution_convert_fusion
  272.8 0.1 stack.25
  272.9 0.1 stack.24
  273.0 6.6 fusion.107
  279.6 0.3 fusion.66
  280.0 1.0 fusion.104
  281.1 0.9 copy.87
  282.0 127.6 %reduce-scatter.6.cloned.1.call-done = bf16[64,8192]{1,0:T(8,128)(2,1)} async-done(((bf16[1024,8192]{1,0:T(8,128)(2,1)}), bf16[64,8192]{1,0:T(8,128)(2,1)}) %reduce-scatter.6.cloned.1.call-update) | async-done | bytes 1048592 | tf_op jit(solution)/shard_map/reduce_scatter | solution.py:33
  409.6 1.6 split.28
  411.2 1.9 split.29
  413.1 101.0 %reduce-scatter.8.cloned.1.call-done = bf16[256,1024]{1,0:T(8,128)(2,1)} async-done(((bf16[4096,1024]{1,0:T(8,128)(2,1)}), bf16[256,1024]{1,0:T(8,128)(2,1)}) %reduce-scatter.8.cloned.1.call-update) | async-done | bytes 524304 | tf_op jit(solution)/shard_map/reduce_scatter | solution.py:227
  514.1 0.3 all-gather.10.cloned.1.call-start
  514.3 1.8 split.27
  516.1 5.6 fusion.39
  521.8 60.3 %reduce-scatter.10.cloned.1.call-done = bf16[64,12]{1,0:T(8,128)(2,1)} async-done(((bf16[1024,12]{1,0:T(8,128)(2,1)}), bf16[64,12]{1,0:T(8,128)(2,1)}) %reduce-scatter.10.cloned.1.call-update) | async-done | bytes 1552
  582.1 0.8 copy.88
  582.8 19.0 %psum.31 = bf16[12,64]{1,0:T(8,128)(2,1)S(1)} all-reduce(bf16[12,64]{1,0:T(8,128)(2,1)S(1)} %copy.88), channel_id=1, replica_groups=mesh['dp'=8,'zero'=16] {'dp'}, use_global_device_ids=true, to_apply=%region_26.27 | all-reduce | flops 768 | bytes 3072 | tf_op jit(solution)/shard_map/psum | solution.py:239
  601.8 0.6 multiply_subtract_fusion.4
  602.5 60.1 %all-reduce.3.cloned.1.call-done = (bf16[64,1024]{1,0:T(8,128)(2,1)}, bf16[64,4096]{1,0:T(8,128)(2,1)}, bf16[256,1024]{1,0:T(8,128)(2,1)}) async-done(((bf16[64,1024]{1,0:T(8,128)(2,1)}, bf16[64,4096]{1,0:T(8,128)(2,1)}, bf16[256,1024]{1,0:T(8,128)(2,1)}), (bf16[64,1024]{1,0:T(8,128)(2,1)}, bf16[64,4096]{1,0:T(8,128)(2,1)}, bf16[256,1024]{1,0:T(8,128)(2,1)})) %all-reduce.3.cloned.1.call-update) | async-done | bytes 1179664 | tf_op jit(solution)/shard_map/psum | solution.py:236
  662.5 2.3 multiply_subtract_fusion.3
  664.9 4.4 multiply_subtract_fusion
  669.2 2.6 multiply_subtract_fusion.1
  671.9 36.7 %all-gather.10.cloned.1.call-done = bf16[512,3072]{1,0:T(8,128)(2,1)} async-done(((bf16[64,3072]{1,0:T(8,128)(2,1)}), bf16[512,3072]{1,0:T(8,128)(2,1)}) %all-gather.10.cloned.1.call-update) | async-done | bytes 3145744 | tf_op jit(solution)/shard_map/all_gather | solution.py:235
  708.6 2.4 reduce_sum.197
  711.0 2.1 multiply_subtract_fusion.2
  (96 shorter events, 1.0 us)
Async XLA Ops:
  7.2 2.4 copy-start.15
  7.2 2.4 copy-start.9
  7.2 2.5 copy-start.7
  7.2 79.7 %all-gather.8.cloned.1.call-start = ((), (), s32[]{:S(2)}) async-start(), calls=%async_computation.4 | async-start | bytes 8912896 | tf_op jit(solution)/shard_map/all_gather | solution.py:204
  9.5 187.5 %all-gather.6.cloned.1.call-start = ((), (), s32[]{:S(2)}) async-start(), calls=%async_computation.3 | async-start | bytes 17825792 | tf_op jit(solution)/shard_map/all_gather | solution.py:22
  9.7 1.2 copy-start.27
  9.8 27.4 %copy-start.1 = (bf16[128,1024]{1,0:T(8,128)(2,1)S(1)}, bf16[128,1024]{1,0:T(8,128)(2,1)}, u32[]{:S(2)}) copy-start(bf16[128,1024]{1,0:T(8,128)(2,1)} %param.18) | copy-start | bytes 786436
  9.8 27.7 %copy-start.30 = (s32[1,128]{1,0:T(1,128)S(1)}, s32[1,128]{1,0:T(1,128)}, u32[]{:S(2)}) copy-start(s32[1,128]{1,0:T(1,128)} %param.20) | copy-start | bytes 1540
  9.8 77.2 %copy-start.2 = (bf16[128,1024]{1,0:T(8,128)(2,1)S(1)}, bf16[128,1024]{1,0:T(8,128)(2,1)}, u32[]{:S(2)}) copy-start(bf16[128,1024]{1,0:T(8,128)(2,1)} %param.19) | copy-start | bytes 786436
  10.9 398.8 %reduce-scatter.6.cloned.1.call-start = ((), (), s32[]{:S(2)}) async-start(), calls=%async_computation.5 | async-start | bytes 17825792 | tf_op jit(solution)/shard_map/reduce_scatter | solution.py:33
  202.8 4.9 copy-start.18
  204.0 6.4 copy-start.21
  205.5 1.0 copy-start.16
  220.9 6.8 copy-start.13
  227.9 15.0 %copy-start.4 = (f32[128,1024]{1,0:T(8,128)}, f32[128,1024]{1,0:T(8,128)S(1)}, u32[]{:S(2)}) copy-start(f32[128,1024]{1,0:T(8,128)S(1)} %get-tuple-element.55) | copy-start | bytes 1572868
  230.6 6.2 copy-start.20
  230.8 0.7 copy-start.22
  231.5 8.1 %copy-start.19 = (bf16[128,1024]{0,1:T(8,128)(2,1)S(1)}, bf16[128,1024]{0,1:T(8,128)(2,1)}, u32[]{:S(2)}) copy-start(bf16[128,1024]{0,1:T(8,128)(2,1)} %copy-done.18) | copy-start | bytes 786436
  235.8 1.0 copy-start.17
  239.6 6.5 copy-start.14
  254.7 3.6 copy-start
  264.9 1.6 copy-start.3
  264.9 249.1 %reduce-scatter.8.cloned.1.call-start = ((), (), s32[]{:S(2)}) async-start(), calls=%async_computation.6 | async-start | bytes 8912896 | tf_op jit(solution)/shard_map/reduce_scatter | solution.py:227
  272.7 309.4 %reduce-scatter.10.cloned.1.call-start = ((), (), s32[]{:S(2)}) async-start(), calls=%async_computation.8 | async-start | bytes 278528
  273.0 6.9 copy-start.5
  282.0 380.6 %all-reduce.3.cloned.1.call-start = ((), (), s32[]{:S(2)}) async-start(), calls=%async_computation.9 | async-start | bytes 2359296 | tf_op jit(solution)/shard_map/psum | solution.py:236
  514.1 194.5 %all-gather.10.cloned.1.call-start = ((), (), s32[]{:S(2)}) async-start(), calls=%async_computation.7 | async-start | bytes 3538944 | tf_op jit(solution)/shard_map/all_gather | solution.py:235
  516.1 85.7 %copy-start.28 = (f32[12,64]{1,0:T(8,128)S(1)}, f32[12,64]{1,0:T(8,128)}, u32[]{:S(2)}) copy-start(f32[12,64]{1,0:T(8,128)} %param.30) | copy-start | bytes 9220
  516.1 85.7 %copy-start.29 = (f32[12,64]{1,0:T(8,128)S(1)}, f32[12,64]{1,0:T(8,128)}, u32[]{:S(2)}) copy-start(f32[12,64]{1,0:T(8,128)} %param.35) | copy-start | bytes 9220
  521.8 143.0 %copy-start.6 = (f32[256,1024]{1,0:T(8,128)S(1)}, f32[256,1024]{1,0:T(8,128)}, u32[]{:S(2)}) copy-start(f32[256,1024]{1,0:T(8,128)} %param.24) | copy-start | bytes 3145732
  662.5 2.3 copy-start.26
  664.8 4.4 copy-start.8
  664.8 4.4 copy-start.11
  664.8 4.4 copy-start.12
  664.8 4.4 copy-start.25
  671.9 39.1 %copy-start.10 = (f32[64,3072]{1,0:T(8,128)S(1)}, f32[64,3072]{1,0:T(8,128)}, u32[]{:S(2)}) copy-start(f32[64,3072]{1,0:T(8,128)} %param.21) | copy-start | bytes 2359300
  671.9 39.1 %copy-start.23 = (f32[64,3072]{1,0:T(8,128)S(1)}, f32[64,3072]{1,0:T(8,128)}, u32[]{:S(2)}) copy-start(f32[64,3072]{1,0:T(8,128)} %param.26) | copy-start | bytes 2359300
  671.9 39.1 %copy-start.24 = (f32[64,3072]{1,0:T(8,128)S(1)}, f32[64,3072]{1,0:T(8,128)}, u32[]{:S(2)}) copy-start(f32[64,3072]{1,0:T(8,128)} %param.31) | copy-start | bytes 2359300
Sparse Core Ops, SparseCore 0:
  11.1 75.7 all-gather.7
  90.0 107.0 all-gather.5
  265.0 144.5 reduce-scatter.5
  413.8 100.2 reduce-scatter.7
  518.1 63.8 reduce-scatter.9
  585.8 76.7 all-reduce.2
  664.8 43.7 all-gather.9
